TPU v7x, 256 devices: a whole 4x4x8 slice. The times are simulated.
256 devices in a mesh: dp: 64 (over z, y, x_hi), mp: 4 (over x_lo, core).
Axes of the slice: x: 4 (x_hi: 2, x_lo: 2; x = x_hi * 2 + x_lo), y: 4, z: 8, core: 2. Of those that a mesh axis runs over, the one named last changes fastest.
Arguments:
- hidden_states: bfloat16 [32768, 3584], P('dp'), may hold values from -6 to 6
- token_ids: int32 [2048, 16], P('dp'), may hold values from 0 to 152063, as said below
- norm_gain: float32 [3584], replicated, may hold values from 0.5 to 1.5
- q_weight: bfloat16 [3584, 3584], P('dp', 'mp'), may hold values from -0.09375 to 0.09375
- key_matrix: bfloat16 [3584, 512], P('dp', 'mp'), may hold values from -0.09375 to 0.09375
- value_matrix: bfloat16 [3584, 512], P('dp', 'mp'), may hold values from -0.09375 to 0.09375
- out_weight: bfloat16 [3584, 3584], P('dp', 'mp'), may hold values from -0.09375 to 0.09375
- label_table: bfloat16 [65536, 3584], P(('dp', 'mp')), may hold values from -6 to 6
- refresh_rows: int32 [2048], P(('dp', 'mp')), may hold values from 0 to 255, as said below
- label_counts: int32 [65536], P(('dp', 'mp')), may hold values from 1 to 8191
- queries: bfloat16 [128, 3584], replicated, may hold values from -6 to 6
- positives: int32 [128, 8], replicated, may hold values from 0 to 65535
Outputs:
- label_grad: float32 [65536, 3584], P(('dp', 'mp'))
- query_grad: float32 [128, 3584], replicated
- loss: float32 [], replicated
Inputs may be any that keep to these rules, and one draw needn't show every extreme that they name: `token_ids`: in every text the first id is not 0, and after an id 0 all later ids of that text are 0. `refresh_rows`: the 8 entries of each aligned block of 8 entries are distinct.
All inputs are finite; a program needn't handle non-finite values.
Results may differ from a plain program's by a relative error of at most 0.003.
Values may be sent and summed in bfloat16 or wider, within the bound.
No kernel may reach another device: no remote copies, remote signals or barrier semaphores. Data moves between devices by JAX's collectives and lax.ppermute only.
A program may use at most 128 MiB of HBM per device.

v0:
```python
import math
import jax
import jax.numpy as jnp
from jax import lax
from jax.sharding import PartitionSpec as P

HEAD_WIDTH = 128
rope_theta = 1000000.0
norm_eps = 1e-06
focal_beta = 0.9999


def rotary(values, head_size):
    length = values.shape[1]
    half = head_size // 2
    frequency = rope_theta ** (-2.0 * jnp.arange(half, dtype=jnp.float32) / head_size)
    angles = jnp.arange(length, dtype=jnp.float32)[:, None] * frequency[None, :]
    cosine = jnp.concatenate([jnp.cos(angles), jnp.cos(angles)], axis=1)[None, :, None, :]
    sine = jnp.concatenate([jnp.sin(angles), jnp.sin(angles)], axis=1)[None, :, None, :]
    turned = jnp.concatenate([-values[..., half:], values[..., :half]], axis=-1)
    return values * cosine + turned * sine


def attend(query_rows, key_rows, value_rows, text_ids, head_size):
    texts, length = text_ids.shape
    kv_heads = key_rows.shape[1] // head_size
    repeat = query_rows.shape[1] // head_size // kv_heads
    query_r = query_rows.reshape(texts, length, kv_heads, repeat, head_size)
    key_r = key_rows.reshape(texts, length, kv_heads, head_size)
    value_r = value_rows.reshape(texts, length, kv_heads, head_size)
    scores = jnp.einsum(
        "ntgrd,nsgd->ngrts", query_r, key_r, preferred_element_type=jnp.float32
    ) / math.sqrt(head_size)
    causal = jnp.arange(length)[:, None] >= jnp.arange(length)[None, :]
    allowed = causal[None, None, None, :, :] & (text_ids != 0)[:, None, None, None, :]
    weights = jnp.where(allowed, jnp.exp(scores), 0.0)
    probs = (weights / jnp.sum(weights, axis=-1, keepdims=True)).astype(jnp.bfloat16)
    mixed = jnp.einsum("ngrts,nsgd->ntgrd", probs, value_r, preferred_element_type=jnp.float32)
    return mixed.reshape(texts * length, -1).astype(jnp.bfloat16)


def shards(
    hidden_states,
    token_ids,
    norm_gain,
    q_weight,
    key_matrix,
    value_matrix,
    out_weight,
    label_table,
    refresh_rows,
    label_counts,
    queries,
    positives,
):
    width = hidden_states.shape[1]
    group_tokens = hidden_states.shape[0]
    texts, length = token_ids.shape
    states = hidden_states.astype(jnp.float32)
    scaled = lax.rsqrt(jnp.mean(states * states, axis=1, keepdims=True) + norm_eps)
    normed = (states * scaled * norm_gain).astype(jnp.bfloat16)
    pieces = (
        lax.all_gather(q_weight, "dp", axis=0, tiled=True),
        lax.all_gather(key_matrix, "dp", axis=0, tiled=True),
        lax.all_gather(value_matrix, "dp", axis=0, tiled=True),
    )
    query_raw, key_raw, value_raw = tuple(
        (jnp.dot(normed, piece, preferred_element_type=jnp.float32) for piece in pieces)
    )
    queries_rot = (
        rotary(query_raw.reshape(texts, length, -1, HEAD_WIDTH), HEAD_WIDTH)
        .reshape(group_tokens, -1)
        .astype(jnp.bfloat16)
    )
    rotary_keys = (
        rotary(key_raw.reshape(texts, length, -1, HEAD_WIDTH), HEAD_WIDTH)
        .reshape(group_tokens, -1)
        .astype(jnp.bfloat16)
    )
    values_rot = value_raw.astype(jnp.bfloat16)
    attended = attend(queries_rot, rotary_keys, values_rot, token_ids, HEAD_WIDTH)
    live = (token_ids != 0).astype(jnp.float32)
    share = texts // lax.axis_size("mp")
    member = lax.axis_index("mp")
    live_own = lax.dynamic_slice_in_dim(live, member * share, share, 0)
    states_own = lax.dynamic_slice_in_dim(
        states, member * share * length, share * length, 0
    ).reshape(share, length, width)
    counted = jnp.sum(live_own, axis=1, keepdims=True)
    head_terms = lax.dot_general(
        attended,
        lax.all_gather(out_weight, "dp", axis=0, tiled=True),
        (((1,), (1,)), ((), ())),
        preferred_element_type=jnp.float32,
    )
    output_own = lax.psum_scatter(head_terms, "mp", scatter_dimension=0, tiled=True).reshape(
        share, length, width
    )
    refreshed = (
        jnp.sum((states_own + output_own) * live_own[:, :, None], axis=1) / counted
    ).astype(jnp.bfloat16)
    table = label_table.at[refresh_rows].set(refreshed)
    root = math.sqrt(width)
    owned = label_table.shape[0]
    logits = (
        lax.dot_general(
            queries, table, (((1,), (1,)), ((), ())), preferred_element_type=jnp.float32
        )
        / root
    )
    first_label = (lax.axis_index("dp") * lax.axis_size("mp") + member) * owned
    label_ids = first_label + jnp.arange(owned, dtype=jnp.int32)
    matched = jnp.any(positives[:, :, None] == label_ids[None, None, :], axis=1)
    signs = jnp.where(matched, 1.0, -1.0)
    margin = signs * logits
    balance = (1.0 - focal_beta) / -jnp.expm1(
        label_counts.astype(jnp.float32) * math.log(focal_beta)
    )
    missed = jax.nn.sigmoid(-margin)
    softened = jax.nn.softplus(-margin)
    focal_terms = balance[None, :] * missed * missed * softened
    slopes = (
        balance[None, :]
        * signs
        * (-(missed * missed) * (2.0 * jax.nn.sigmoid(margin) * softened + missed))
    ).astype(jnp.bfloat16)
    query_part = jnp.dot(slopes, table, preferred_element_type=jnp.float32) / root
    label_part = (
        lax.dot_general(
            slopes, queries, (((0,), (0,)), ((), ())), preferred_element_type=jnp.float32
        )
        / root
    )
    query_sum, loss_sum, summed_weight = lax.psum(
        (query_part, jnp.sum(focal_terms), jnp.sum(balance)), ("dp", "mp")
    )
    total_labels = owned * lax.axis_size("dp") * lax.axis_size("mp")
    factor = total_labels / summed_weight
    loss = factor * loss_sum / (queries.shape[0] * total_labels)
    return (factor * label_part, factor * query_sum, loss)


def solution(mesh):
    in_specs = (
        P("dp", None),
        P("dp", None),
        P(),
        P("dp", "mp"),
        P("dp", "mp"),
        P("dp", "mp"),
        P("dp", "mp"),
        P(("dp", "mp"), None),
        P(("dp", "mp")),
        P(("dp", "mp")),
        P(),
        P(),
    )
    out_specs = (P(("dp", "mp"), None), P(), P())
    return jax.shard_map(shards, mesh=mesh, in_specs=in_specs, out_specs=out_specs, check_vma=False)
```

profile of v0, /device:TPU:2, one launch (start us, length us, event | category | flops | bytes accessed | tf_op | source)
XLA Modules:
  0.0 762.3 jit_solution(14979798838357729430)
XLA Ops:
  7.2 0.0 copy-start
  7.2 0.0 copy-start.6
  7.2 0.0 all-gather.3.cloned.1.call-start
  7.2 0.0 copy-start.4
  7.2 0.7 all-gather.3.cloned.1.call-update
  7.9 0.0 all-gather.5.cloned.1.call-start
  8.0 0.7 all-gather.5.cloned.1.call-update
  8.7 0.0 reduce-scatter.2.cloned.1.call-start
  8.7 0.0 copy-done.6
  8.7 0.1 copy.28
  8.8 0.1 fusion.18
  8.9 0.1 pad_maximum_fusion
  9.0 3.0 multiply_reduce_fusion
  12.0 0.0 copy-done.4
  12.0 190.2 %all_gather.13 = bf16[3584,128]{1,0:T(8,128)(2,1)S(1)} all-gather(bf16[56,128]{1,0:T(8,128)(2,1)S(1)} %copy-done.4), channel_id=1, replica_groups=mesh['dp'=64,'mp'=4] {'dp'}, dimensions={0}, use_global_device_ids=true | all-gather | bytes 931840 | tf_op jit(solution)/shard_map/all_gather | solution.py:64
  202.2 0.0 copy-done.1
  202.2 0.0 copy-done.9
  202.2 1.2 fusion.23
  203.4 0.1 slice_negate_fusion.1
  203.5 0.1 fusion.10
  203.7 0.1 broadcast_and_fusion
  203.8 0.0 copy-done.5
  203.8 180.0 %all_gather.12 = bf16[3584,128]{1,0:T(8,128)(2,1)S(1)} all-gather(bf16[56,128]{1,0:T(8,128)(2,1)S(1)} %copy-done.5), channel_id=1, replica_groups=mesh['dp'=64,'mp'=4] {'dp'}, dimensions={0}, use_global_device_ids=true | all-gather | bytes 931840 | tf_op jit(solution)/shard_map/all_gather | solution.py:65
  383.8 1.2 convolution_convert_fusion.1
  385.0 0.0 all-gather.3.cloned.1.call-done
  385.0 9.2 %fusion.22 = f32[512,896]{1,0:T(8,128)} fusion(bf16[3584,896]{1,0:T(8,128)(2,1)} %all-gather.3.cloned.1.call-done, f32[3584]{0:T(1024)S(1)} %copy-done.9, f32[512]{0:T(512)S(1)} %add_rsqrt_fusion, bf16[512,3584]{1,0:T(8,128)(2,1)} %param.12), kind=kOutput, calls=%fused_computation.58 | convolution fusion | flops 3295674368 | bytes 11943936 | tf_op jit(solution)/shard_map/dot_general | solution.py:68
  394.2 1.6 reshape.123
  395.8 0.8 slice_negate_fusion
  396.5 0.6 maximum_multiply_fusion
  397.2 0.0 copy-start.3
  397.2 0.2 mul.215
  397.4 1.3 copy-done.3
  398.7 1.0 fusion
  399.7 1.0 reshape.124
  400.7 2.0 fusion.25
  402.8 0.5 fusion.1
  403.2 0.3 copy.31
  403.5 0.0 all-gather.5.cloned.1.call-done
  403.6 8.9 %fusion.4 = f32[512,3584]{1,0:T(8,128)} fusion(bf16[3584,896]{1,0:T(8,128)(2,1)} %all-gather.5.cloned.1.call-done, bf16[64,8,7,128]{3,2,1,0:T(8,128)(2,1)S(1)} %bitcast.69), kind=kOutput, calls=%fused_computation.21 | convolution fusion | flops 3288334336 | bytes 14680064 | tf_op jit(solution)/shard_map/dot_general | solution.py:90
  412.4 0.0 reduce-scatter.2.cloned.1.call-update
  412.5 0.3 all-reduce.3.cloned.1.call-start
  412.7 0.0 copy-start.7
  412.8 0.0 copy-start.10
  412.8 0.0 copy-start.8
  412.8 6.0 convert_element_type.43
  418.8 0.1 dynamic-slice_convert_fusion
  418.9 0.1 copy.32
  419.0 0.0 copy-done.7
  419.0 0.1 copy.26
  419.1 0.4 compare_reduce_fusion
  419.5 0.1 copy.27
  419.6 0.1 fusion.19
  419.7 0.0 copy-done.10
  419.7 0.6 fusion.24
  420.3 60.5 %reduce-scatter.2.cloned.1.call-done = f32[128,3584]{1,0:T(8,128)} async-done(((f32[512,3584]{1,0:T(8,128)}), f32[128,3584]{1,0:T(8,128)}) %reduce-scatter.2.cloned.1.call-update) | async-done | bytes 1835024 | tf_op jit(solution)/shard_map/reduce_scatter | solution.py:96
  480.9 2.5 multiply_reduce_fusion.1
  483.4 1.8 scatter_custom_fusion
  485.3 1.3 fusion.14
  486.6 1.8 convolution_multiply_fusion.1
  488.4 0.0 all-reduce.3.cloned.1.call-update
  488.4 78.1 %all-reduce = (f32[]{:T(128)}, f32[]{:T(128)}) all-reduce(f32[]{:T(128)} %get-tuple-element.5, f32[]{:T(128)} %get-tuple-element.15), channel_id=1, replica_groups=mesh['dp'=64,'mp'=4] {'dp','mp'}, use_global_device_ids=true, to_apply=%region_8.9 | all-reduce | flops 2 | bytes 16 | tf_op jit(solution)/shard_map/psum | solution.py:134
  567.8 2.6 convolution_multiply_fusion
  570.4 181.4 %all-reduce.3.cloned.1.call-done = f32[128,3584]{1,0:T(8,128)} async-done(((f32[128,3584]{1,0:T(8,128)}), f32[128,3584]{1,0:T(8,128)}) %all-reduce.3.cloned.1.call-update) | async-done | bytes 1835024 | tf_op jit(solution)/shard_map/psum | solution.py:134
  751.8 2.9 broadcast_multiply_fusion
  (13 shorter events, 0.1 us)
Async XLA Ops:
  7.2 478.1 %copy-start = (bf16[128,3584]{1,0:T(8,128)(2,1)S(1)}, bf16[128,3584]{1,0:T(8,128)(2,1)}, u32[]{:S(2)}) copy-start(bf16[128,3584]{1,0:T(8,128)(2,1)} %param.22) | copy-start | bytes 2752516
  7.2 1.5 copy-start.6
  7.2 377.8 %all-gather.3.cloned.1.call-start = ((), (), s32[]{:S(2)}) async-start(), calls=%async_computation.1 | async-start | bytes 6522880 | tf_op jit(solution)/shard_map/all_gather | solution.py:63
  7.2 4.8 copy-start.4
  7.9 395.6 %all-gather.5.cloned.1.call-start = ((), (), s32[]{:S(2)}) async-start(), calls=%async_computation.2 | async-start | bytes 6522880 | tf_op jit(solution)/shard_map/all_gather | solution.py:92
  8.7 472.2 %reduce-scatter.2.cloned.1.call-start = ((), (), s32[]{:S(2)}) async-start(), calls=%async_computation.3 | async-start | bytes 9175040 | tf_op jit(solution)/shard_map/reduce_scatter | solution.py:96
  9.0 193.2 %copy-start.1 = (bf16[512,3584]{1,0:T(8,128)(2,1)S(1)}, bf16[512,3584]{1,0:T(8,128)(2,1)}, u32[]{:S(2)}) copy-start(bf16[512,3584]{1,0:T(8,128)(2,1)} %param.12) | copy-start | bytes 11010052
  9.0 193.2 %copy-start.9 = (f32[3584]{0:T(1024)S(1)}, f32[3584]{0:T(1024)}, u32[]{:S(2)}) copy-start(f32[3584]{0:T(1024)} %param.14) | copy-start | bytes 43012
  202.2 1.6 copy-start.5
  397.2 1.5 copy-start.3
  412.5 339.3 %all-reduce.3.cloned.1.call-start = ((), (), s32[]{:S(2)}) async-start(), calls=%async_computation.4 | async-start | bytes 3670016 | tf_op jit(solution)/shard_map/psum | solution.py:134
  412.7 6.2 copy-start.7
  412.8 6.9 copy-start.10
  412.8 6.9 copy-start.8
  418.8 64.6 %copy-start.2 = (bf16[256,3584]{1,0:T(8,128)(2,1)S(1)}, bf16[256,3584]{1,0:T(8,128)(2,1)}, u32[]{:S(2)}) copy-start(bf16[256,3584]{1,0:T(8,128)(2,1)} %param.19) | copy-start | bytes 5505028
Sparse Core Ops, SparseCore 0:
  11.7 146.0 all-gather.2
  161.5 139.9 all-gather.4
  412.6 68.2 reduce-scatter.1
  488.6 263.1 all-reduce.2
where the time goes:
time: 763 us; the launch traced here: 762 us
  blocking collectives  448 us (59%)
  waiting for transfers between devices  243 us (32%)
  matrix products  28.6 us (4%)
  other arithmetic  20.5 us (3%)
  between operations  16.5 us (2%)
    all_gather x1, blocking collectives, shards(): lax.all_gather(key_matrix, 'dp', axis=0, tiled=True)  190 us
    psum x1, waiting for transfers between devices, shards(): lax.psum((query_part, jnp.sum(focal_terms), jnp.sum(balance)), ('dp', 'mp'))  181 us
    all_gather x1, blocking collectives, shards(): lax.all_gather(value_matrix, 'dp', axis=0, tiled=True)  180 us
    psum x1, blocking collectives, shards(): lax.psum((query_part, jnp.sum(focal_terms), jnp.sum(balance)), ('dp', 'mp'))  78.1 us
    reduce_scatter x1, waiting for transfers between devices, shards(): lax.psum_scatter(head_terms, 'mp', scatter_dimension=0, tiled=True)  60.5 us
  transfers between devices with their start and end apart: 4, of which 2 were waited for; matrix products, arithmetic and copies ran while one was open for 4% of the time, Pallas kernels for 0%

commit v1 on v0

--- a/solution.py
+++ b/solution.py
@@ -132,7 +132,7 @@
         / root
     )
     query_sum, loss_sum, summed_weight = lax.psum(
-        (query_part, jnp.sum(focal_terms), jnp.sum(balance)), ("dp", "mp")
+        lax.psum((query_part, jnp.sum(focal_terms), jnp.sum(balance)), "dp"), "mp"
     )
     total_labels = owned * lax.axis_size("dp") * lax.axis_size("mp")
     factor = total_labels / summed_weight

time: 763 us -> 1380 us (1.81)
  waiting for transfers between devices: 243 us -> 753 us
  blocking collectives: 448 us -> 557 us
    psum x1 -> x2, waiting for transfers between devices: 181 us -> 691 us  [the longest x1 691 us: shards(): lax.psum((query_part, jnp.sum(focal_terms), jnp.sum(balance)), 'dp')]
    psum x1 -> x2, blocking collectives: 78.1 us -> 187 us  [the longest x1 180 us: shards(): lax.psum((query_part, jnp.sum(focal_terms), jnp.sum(balance)), 'dp')]
  transfers between devices with their start and end apart: 4 -> 5, of which waited for: 2 -> 2; matrix products, arithmetic and copies ran while one was open for 4% -> 2% of each run, Pallas kernels for 0% -> 0%
where the time goes in v1:
time: 1380 us
  waiting for transfers between devices  753 us (55%)
  blocking collectives  557 us (40%)
  matrix products  28.6 us (2%)
  other arithmetic  20.5 us (1%)
  between operations  16.5 us (1%)
    psum x1, waiting for transfers between devices, shards(): lax.psum((query_part, jnp.sum(focal_terms), jnp.sum(balance)), 'dp')  691 us
    all_gather x1, blocking collectives, shards(): lax.all_gather(key_matrix, 'dp', axis=0, tiled=True)  190 us
    psum x1, blocking collectives, shards(): lax.psum((query_part, jnp.sum(focal_terms), jnp.sum(balance)), 'dp')  180 us
    all_gather x1, blocking collectives, shards(): lax.all_gather(value_matrix, 'dp', axis=0, tiled=True)  180 us
    reduce_scatter x1, waiting for transfers between devices, shards(): lax.psum_scatter(head_terms, 'mp', scatter_dimension=0, tiled=True)  60.5 us
  transfers between devices with their start and end apart: 5, of which 2 were waited for; matrix products, arithmetic and copies ran while one was open for 2% of the time, Pallas kernels for 0%

profile of v1, /device:TPU:2, one launch (start us, length us, event | category | flops | bytes accessed | tf_op | source)
XLA Modules:
  0.0 1380.2 jit_solution(5247569565405925225)
XLA Ops:
  7.2 0.0 copy-start
  7.2 0.0 copy-start.6
  7.2 0.0 all-gather.3.cloned.1.call-start
  7.2 0.0 copy-start.4
  7.2 0.7 all-gather.3.cloned.1.call-update
  7.9 0.0 all-gather.5.cloned.1.call-start
  8.0 0.7 all-gather.5.cloned.1.call-update
  8.7 0.0 reduce-scatter.2.cloned.1.call-start
  8.7 0.0 copy-done.6
  8.7 0.1 copy.28
  8.8 0.1 fusion.18
  8.9 0.1 pad_maximum_fusion
  9.0 3.0 multiply_reduce_fusion
  12.0 0.0 copy-done.4
  12.0 190.2 %all_gather.13 = bf16[3584,128]{1,0:T(8,128)(2,1)S(1)} all-gather(bf16[56,128]{1,0:T(8,128)(2,1)S(1)} %copy-done.4), channel_id=1, replica_groups=mesh['dp'=64,'mp'=4] {'dp'}, dimensions={0}, use_global_device_ids=true | all-gather | bytes 931840 | tf_op jit(solution)/shard_map/all_gather | solution.py:64
  202.2 0.0 copy-done.1
  202.2 1.2 fusion.23
  203.4 0.1 slice_negate_fusion.1
  203.5 0.1 fusion.10
  203.7 0.1 broadcast_and_fusion
  203.8 180.0 %all_gather.12 = bf16[3584,128]{1,0:T(8,128)(2,1)S(1)} all-gather(bf16[56,128]{1,0:T(8,128)(2,1)S(1)} %copy-done.5), channel_id=1, replica_groups=mesh['dp'=64,'mp'=4] {'dp'}, dimensions={0}, use_global_device_ids=true | all-gather | bytes 931840 | tf_op jit(solution)/shard_map/all_gather | solution.py:65
  383.8 1.2 convolution_convert_fusion.1
  385.0 0.0 all-gather.3.cloned.1.call-done
  385.0 9.2 fusion.22
  394.2 1.6 reshape.123
  395.8 0.8 slice_negate_fusion
  396.5 0.6 maximum_multiply_fusion
  397.2 0.0 copy-start.3
  397.2 0.2 mul.215
  397.4 1.3 copy-done.3
  398.7 1.0 fusion
  399.7 1.0 reshape.124
  400.7 2.0 fusion.25
  402.8 0.5 fusion.1
  403.2 0.3 copy.31
  403.5 0.0 all-gather.5.cloned.1.call-done
  403.6 8.9 fusion.4
  412.4 0.0 reduce-scatter.2.cloned.1.call-update
  412.5 0.3 all-reduce.5.cloned.1.call-start
  412.7 0.0 copy-start.7
  412.8 0.0 copy-start.10
  412.8 0.0 copy-start.8
  412.8 6.0 convert_element_type.43
  418.8 0.1 dynamic-slice_convert_fusion
  418.9 0.1 copy.32
  419.0 0.1 copy.26
  419.1 0.4 compare_reduce_fusion
  419.5 0.1 copy.27
  419.6 0.1 fusion.19
  419.7 0.0 copy-done.8
  419.7 0.6 fusion.24
  420.3 60.5 %reduce-scatter.2.cloned.1.call-done = f32[128,3584]{1,0:T(8,128)} async-done(((f32[512,3584]{1,0:T(8,128)}), f32[128,3584]{1,0:T(8,128)}) %reduce-scatter.2.cloned.1.call-update) | async-done | bytes 1835024 | tf_op jit(solution)/shard_map/reduce_scatter | solution.py:96
  480.9 2.5 multiply_reduce_fusion.1
  483.4 1.8 scatter_custom_fusion
  485.3 1.3 fusion.14
  486.6 1.8 convolution_multiply_fusion.1
  488.4 0.0 all-reduce.5.cloned.1.call-update
  488.4 0.0 all-reduce.7.cloned.1.call-start
  488.5 690.6 %all-reduce.5.cloned.1.call-done = f32[128,3584]{1,0:T(8,128)} async-done(((f32[128,3584]{1,0:T(8,128)}), f32[128,3584]{1,0:T(8,128)}) %all-reduce.5.cloned.1.call-update) | async-done | bytes 1835024 | tf_op jit(solution)/shard_map/psum | solution.py:135
  1179.1 0.0 all-reduce.7.cloned.1.call-update
  1179.1 180.4 %all-reduce = (f32[]{:T(128)}, f32[]{:T(128)}) all-reduce(f32[]{:T(128)} %get-tuple-element.7, f32[]{:T(128)} %get-tuple-element.17), channel_id=1, replica_groups=mesh['dp'=64,'mp'=4] {'dp'}, use_global_device_ids=true, to_apply=%region_8.9 | all-reduce | flops 2 | bytes 16 | tf_op jit(solution)/shard_map/psum | solution.py:135
  1359.5 6.3 all-reduce.1
  1367.1 2.6 convolution_multiply_fusion
  1369.7 2.9 broadcast_multiply_fusion
  (17 shorter events, 0.1 us)
Async XLA Ops:
  7.2 478.1 %copy-start = (bf16[128,3584]{1,0:T(8,128)(2,1)S(1)}, bf16[128,3584]{1,0:T(8,128)(2,1)}, u32[]{:S(2)}) copy-start(bf16[128,3584]{1,0:T(8,128)(2,1)} %param.22) | copy-start | bytes 2752516
  7.2 1.5 copy-start.6
  7.2 377.8 %all-gather.3.cloned.1.call-start = ((), (), s32[]{:S(2)}) async-start(), calls=%async_computation.1 | async-start | bytes 6522880 | tf_op jit(solution)/shard_map/all_gather | solution.py:63
  7.2 4.8 copy-start.4
  7.9 395.6 %all-gather.5.cloned.1.call-start = ((), (), s32[]{:S(2)}) async-start(), calls=%async_computation.2 | async-start | bytes 6522880 | tf_op jit(solution)/shard_map/all_gather | solution.py:92
  8.7 472.2 %reduce-scatter.2.cloned.1.call-start = ((), (), s32[]{:S(2)}) async-start(), calls=%async_computation.3 | async-start | bytes 9175040 | tf_op jit(solution)/shard_map/reduce_scatter | solution.py:96
  9.0 193.2 %copy-start.1 = (bf16[512,3584]{1,0:T(8,128)(2,1)S(1)}, bf16[512,3584]{1,0:T(8,128)(2,1)}, u32[]{:S(2)}) copy-start(bf16[512,3584]{1,0:T(8,128)(2,1)} %param.12) | copy-start | bytes 11010052
  9.0 193.2 %copy-start.9 = (f32[3584]{0:T(1024)S(1)}, f32[3584]{0:T(1024)}, u32[]{:S(2)}) copy-start(f32[3584]{0:T(1024)} %param.14) | copy-start | bytes 43012
  202.2 1.6 copy-start.5
  397.2 1.5 copy-start.3
  412.5 766.6 %all-reduce.5.cloned.1.call-start = ((), (), s32[]{:S(2)}) async-start(), calls=%async_computation.4 | async-start | bytes 3670016 | tf_op jit(solution)/shard_map/psum | solution.py:135
  412.7 6.2 copy-start.7
  412.8 6.9 copy-start.10
  412.8 6.9 copy-start.8
  418.8 64.6 %copy-start.2 = (bf16[256,3584]{1,0:T(8,128)(2,1)S(1)}, bf16[256,3584]{1,0:T(8,128)(2,1)}, u32[]{:S(2)}) copy-start(bf16[256,3584]{1,0:T(8,128)(2,1)} %param.19) | copy-start | bytes 5505028
  488.4 881.3 %all-reduce.7.cloned.1.call-start = ((), (), s32[]{:S(2)}) async-start(), calls=%async_computation.5 | async-start | bytes 3670016 | tf_op jit(solution)/shard_map/psum | solution.py:134
Sparse Core Ops, SparseCore 0:
  11.7 146.0 all-gather.2
  161.5 139.9 all-gather.4
  412.6 68.2 reduce-scatter.1
  488.6 690.4 all-reduce.4
  1181.8 55.8 all-reduce.6
